TPU v7x, 128 devices: a whole 4x4x4 slice. The times are simulated.
128 devices in a mesh: space: 32 (over y, x, core), snap: 4 (over z).
Axes of the slice: x: 4, y: 4, z: 4, core: 2. Of those that a mesh axis runs over, the one named last changes fastest.
Arguments:
- owned_x: bfloat16 [4096, 128, 512], P('space', None, 'snap'), may hold values from -600 to 600
- owned_y: bfloat16 [4096, 128, 512], P('space', None, 'snap'), may hold values from -6 to 6
- patch_dest: int32 [4096], P('space'), may hold values from -1 to 2047, as said below
Outputs:
- q_basis: float32 [2048, 128, 512], P('space', 'snap')
- r_factor: float32 [512, 512], replicated
- projection: float32 [512, 512], replicated
Inputs may be any that keep to these rules, and one draw needn't show every extreme that they name: `patch_dest`: every row block 0 to 2047 is named by exactly one slot; -1 marks an empty slot. The 128 slots of one owner (one aligned block of 128 slots) name at most 4 row blocks of any one slab d * 64 to (d + 1) * 64 - 1, and some owner names exactly 4 of every slab.
All inputs are finite; a program needn't handle non-finite values.
Results may differ from a plain program's by a relative error of at most 0.0003.
Values may be sent and summed in bfloat16 or wider, within the bound.
A program may use at most 128 MiB of HBM per device.

v0:
```python
import math
import jax
import jax.numpy as jnp
from jax import lax
from jax.sharding import PartitionSpec as P

PATCH = 128
BLK_DEV = 64


def in_order(pieces, dim):
    pieces = jnp.moveaxis(pieces, 0, dim)
    shape = pieces.shape
    return pieces.reshape(*shape[:dim], shape[dim] * shape[dim + 1], *shape[dim + 2 :])


def from_everyone(array, axis):
    copies = jnp.broadcast_to(array, (lax.axis_size(axis), *array.shape))
    return lax.all_to_all(copies, axis, split_axis=0, concat_axis=0, tiled=True)


def collect(array, axis, dim):
    return in_order(from_everyone(array, axis), dim)


def slab_ranks(destination, per_slab):
    target = jnp.where(destination >= 0, destination // per_slab, -1)
    slot_count = destination.shape[-1]
    same_slab = target[..., :, None] == target[..., None, :]
    before = lax.broadcasted_iota(jnp.int32, (slot_count, slot_count), 1) < lax.broadcasted_iota(
        jnp.int32, (slot_count, slot_count), 0
    )
    order_rank = jnp.sum((same_slab & before).astype(jnp.int32), axis=-1)
    return (target, order_rank)


def send_table(destination, per_slab, slab_count, capacity):
    target, order_rank = slab_ranks(destination, per_slab)
    slot_count = destination.shape[0]
    where_to = jnp.where(target >= 0, target * capacity + order_rank, slab_count * capacity)
    start_table = jnp.full((slab_count * capacity,), slot_count, jnp.int32)
    return start_table.at[where_to].set(jnp.arange(slot_count, dtype=jnp.int32), mode="drop")


def arrival_index(all_lists, per_slab, capacity, my_slab):
    slot_count = all_lists.shape[1]
    target, order_rank = slab_ranks(all_lists, per_slab)
    wanted = my_slab * per_slab + jnp.arange(per_slab, dtype=jnp.int32)
    matches = all_lists.reshape(-1)[None, :] == wanted[:, None]
    located = jnp.argmax(matches, axis=1)
    source = located // slot_count
    return source * capacity + order_rank.reshape(-1)[located]


def pick_rows(payload, indices):
    return jnp.take(payload, indices, axis=0, mode="fill", fill_value=0)


def body(owned_x, owned_y, patch_dest):
    slab_count = lax.axis_size("space")
    slot_count = patch_dest.shape[0]
    capacity = slot_count // slab_count
    my_slab = lax.axis_index("space")
    all_lists = collect(patch_dest, "space", 0)
    outgoing_table = send_table(patch_dest, BLK_DEV, slab_count, capacity)
    received_at = arrival_index(
        all_lists.reshape(slab_count, slot_count), BLK_DEV, capacity, my_slab
    )
    rows_total = slab_count * BLK_DEV * PATCH
    contract = (((0,), (0,)), ((), ()))
    block_x, block_y = (
        lax.all_to_all(owned_x, "snap", split_axis=1, concat_axis=2, tiled=True),
        lax.all_to_all(owned_y, "snap", split_axis=1, concat_axis=2, tiled=True),
    )
    width = block_x.shape[-1]
    used = patch_dest >= 0
    kept_x = jnp.where(used[:, None, None], block_x, jnp.zeros_like(block_x))
    local_cross = lax.dot_general(
        kept_x.reshape(-1, width),
        block_y.reshape(-1, width),
        contract,
        preferred_element_type=jnp.float32,
    )
    moved_x = lax.all_to_all(
        pick_rows(block_x, outgoing_table), "space", split_axis=0, concat_axis=0, tiled=True
    )
    slab_x = jnp.take(moved_x, received_at, axis=0)
    cell_rows = slab_x.reshape(-1, width)
    local_gram = lax.dot_general(cell_rows, cell_rows, contract, preferred_element_type=jnp.float32)
    gram_total, cross_total = lax.psum((local_gram, local_cross), ("space", "snap"))
    identity = jnp.eye(width, dtype=jnp.float32)
    lower = jnp.linalg.cholesky(gram_total / rows_total)
    inverse = lax.linalg.triangular_solve(lower, identity, left_side=True, lower=True)
    basis_rows = jnp.dot(cell_rows.astype(jnp.float32), inverse.T, precision=lax.Precision.HIGHEST)
    projection = jnp.dot(inverse, cross_total, precision=lax.Precision.HIGHEST) / math.sqrt(
        rows_total
    )
    return (basis_rows.reshape(slab_x.shape[0], slab_x.shape[1], width), lower.T, projection)


def solution(mesh):
    in_specs = (P("space", None, "snap"), P("space", None, "snap"), P("space"))
    out_specs = (P("space", "snap", None), P(), P())
    return jax.shard_map(body, mesh=mesh, in_specs=in_specs, out_specs=out_specs, check_vma=False)
```

profile of v0, /device:TPU:1, one launch (start us, length us, event | category | flops | bytes accessed | tf_op | source)
XLA Modules:
  0.0 512.7 jit_solution(7003955340530065894)
XLA Ops:
  8.4 8.6 %all-to-all-start = ((s32[32,1,128]{2,1,0:T(1,128)}), s32[32,1,128]{2,1,0:T(1,128)S(1)}, u32[]{:S(2)}, u32[]{:S(2)}) async-start(s32[32,1,128]{2,1,0:T(1,128)} %broadcast_in_dim.58), calls=%async_computation | async-start | bytes 32768 | tf_op jit(solution)/shard_map/all_to_all | solution.py:19
  17.0 6.9 %copy.48 = bf16[128,128,128]{2,0,1:T(8,128)(2,1)} copy(bf16[128,128,128]{2,1,0:T(8,128)(2,1)} %param.3) | data formatting | bytes 8388608 | tf_op args[0]
  23.9 5.0 all-to-all-start.1
  29.0 6.9 %copy.55 = bf16[128,128,128]{2,0,1:T(8,128)(2,1)} copy(bf16[128,128,128]{2,1,0:T(8,128)(2,1)} %param.4) | data formatting | bytes 8388608 | tf_op args[1]
  35.8 42.1 %all-to-all-done.1 = bf16[128,128,128]{2,0,1:T(8,128)(2,1)} async-done(((bf16[128,128,128]{2,0,1:T(8,128)(2,1)}), bf16[128,128,128]{2,0,1:T(8,128)(2,1)}, u32[]{:S(2)}, u32[]{:S(2)}) %all-to-all-start.1) | async-done | bytes 4194336 | tf_op jit(solution)/shard_map/all_to_all | solution.py:72
  84.0 6.4 %copy.50 = bf16[128,32,4,128]{0,3,2,1:T(8,128)(2,1)} copy(bf16[128,32,4,128]{3,0,1,2:T(8,128)(2,1)} %bitcast.6) | data formatting | bytes 8388608 | tf_op jit(solution)/shard_map/all_to_all | solution.py:72
  90.5 7.9 %copy.51 = bf16[128,32,512]{2,1,0:T(8,128)(2,1)} copy(bf16[128,32,512]{0,2,1:T(8,128)(2,1)} %bitcast.79) | data formatting | bytes 8388608 | tf_op jit(solution)/shard_map/all_to_all | solution.py:72
  98.4 5.0 gather_fusion.1
  108.0 22.3 %all-to-all-done.3 = bf16[128,128,128]{2,0,1:T(8,128)(2,1)} async-done(((bf16[128,128,128]{2,0,1:T(8,128)(2,1)}), bf16[128,128,128]{2,0,1:T(8,128)(2,1)}, u32[]{:S(2)}, u32[]{:S(2)}) %all-to-all-start.3) | async-done | bytes 4194336 | tf_op jit(solution)/shard_map/all_to_all | solution.py:73
  130.3 9.6 %all-to-all-start.2 = ((bf16[128,32,512]{2,1,0:T(8,128)(2,1)}), bf16[128,32,512]{2,1,0:T(8,128)(2,1)}, u32[]{:S(2)}, u32[]{:S(2)}) async-start(bf16[128,32,512]{2,1,0:T(8,128)(2,1)} %broadcast_select_fusion.1), calls=%async_computation.2 | async-start | bytes 8388608 | tf_op jit(solution)/shard_map/all_to_all | solution.py:84
  143.4 4.9 copy.49
  152.9 5.4 %copy.56 = bf16[128,4,32,128]{3,1,2,0:T(4,128)(2,1)S(1)} copy(bf16[128,4,32,128]{3,0,2,1:T(8,128)(2,1)} %bitcast.23) | data formatting | bytes 8388608 | tf_op jit(solution)/shard_map/all_to_all | solution.py:73
  161.9 28.7 %all-to-all-done.2 = bf16[128,32,512]{2,1,0:T(8,128)(2,1)} async-done(((bf16[128,32,512]{2,1,0:T(8,128)(2,1)}), bf16[128,32,512]{2,1,0:T(8,128)(2,1)}, u32[]{:S(2)}, u32[]{:S(2)}) %all-to-all-start.2) | async-done | bytes 4194336 | tf_op jit(solution)/shard_map/all_to_all | solution.py:84
  197.4 147.6 %all-reduce.4.cloned.1.call-done = (f32[512,512]{0,1:T(8,128)}, f32[512,512]{1,0:T(8,128)}) async-done(((f32[512,512]{0,1:T(8,128)}, f32[512,512]{1,0:T(8,128)}), (f32[512,512]{0,1:T(8,128)}, f32[512,512]{1,0:T(8,128)})) %all-reduce.4.cloned.1.call-update) | async-done | bytes 2097168 | tf_op jit(solution)/shard_map/psum | solution.py:90
  348.0 11.7 %cholesky.96 = f32[128,128]{1,0:T(8,128)S(1)} custom-call(f32[128,128]{1,0:T(8,128)S(1)} %cholesky.250), custom_call_target="Cholesky" | custom-call | tf_op jit(solution)/shard_map/jit(cholesky)/cholesky | solution.py:92
  359.8 9.8 %custom-call.30 = f32[1,128,128]{1,2,0:T(8,128)S(1)} custom-call(f32[1,128,128]{2,1,0:T(8,128)S(1)} %get-tuple-element.56), custom_call_target="InvertDiagBlocksLowerTriangular" | custom-call | tf_op jit(solution)/shard_map/jit(cholesky)/cholesky | solution.py:92
  372.4 12.1 %cholesky.201 = f32[128,128]{1,0:T(8,128)S(1)} custom-call(f32[128,128]{1,0:T(8,128)S(1)} %cholesky.254), custom_call_target="Cholesky" | custom-call | tf_op jit(solution)/shard_map/jit(cholesky)/cholesky | solution.py:92
  384.5 9.8 %custom-call.31 = f32[1,128,128]{1,2,0:T(8,128)S(1)} custom-call(f32[1,128,128]{2,1,0:T(8,128)S(1)} %get-tuple-element.53), custom_call_target="InvertDiagBlocksLowerTriangular" | custom-call | tf_op jit(solution)/shard_map/jit(cholesky)/cholesky | solution.py:92
  395.9 11.7 %cholesky.222 = f32[128,128]{1,0:T(8,128)S(1)} custom-call(f32[128,128]{1,0:T(8,128)S(1)} %cholesky.259), custom_call_target="Cholesky" | custom-call | tf_op jit(solution)/shard_map/jit(cholesky)/cholesky | solution.py:92
  408.3 9.8 %custom-call.32 = f32[1,128,128]{1,2,0:T(8,128)S(1)} custom-call(f32[1,128,128]{2,1,0:T(8,128)S(1)} %get-tuple-element.50), custom_call_target="InvertDiagBlocksLowerTriangular" | custom-call | tf_op jit(solution)/shard_map/jit(cholesky)/cholesky | solution.py:92
  419.5 11.9 %cholesky.239 = f32[128,128]{1,0:T(8,128)S(1)} custom-call(f32[128,128]{1,0:T(8,128)S(1)} %convolution_subtract_fusion.5), custom_call_target="Cholesky" | custom-call | tf_op jit(solution)/shard_map/jit(cholesky)/cholesky | solution.py:92
  436.5 13.9 %while.1 = (s32[]{:T(128)}, f32[512,512]{1,0:T(8,128)}, s32[4,2]{0,1:T(2,128)S(1)}, f32[4,128,128]{2,1,0:T(8,128)}, s32[]{:T(128)}) while((s32[]{:T(128)}, f32[512,512]{1,0:T(8,128)}, s32[4,2]{0,1:T(2,128)S(1)}, f32[4,128,128]{2,1,0:T(8,128)}, s32[]{:T(128)}) %tuple.41), condition=%wide.while_cond, body=%wide.while_body.sunk | while | flops 2 | bytes 132705 | solution.py:93
  450.4 40.1 %custom-call.33 = f32[4,128,128]{1,2,0:T(8,128)S(1)} custom-call(f32[4,128,128]{2,1,0:T(8,128)} %get-tuple-element.12), custom_call_target="InvertDiagBlocksLowerTriangular" | custom-call | tf_op jit(solution)/shard_map/triangular_solve | solution.py:93
  496.5 5.1 fusion.5
  (92 shorter events, 66.1 us)
Async XLA Ops:
  8.4 15.5 %all-to-all-start = ((s32[32,1,128]{2,1,0:T(1,128)}), s32[32,1,128]{2,1,0:T(1,128)S(1)}, u32[]{:S(2)}, u32[]{:S(2)}) async-start(s32[32,1,128]{2,1,0:T(1,128)} %broadcast_in_dim.58), calls=%async_computation | async-start | bytes 32768 | tf_op jit(solution)/shard_map/all_to_all | solution.py:19
  23.9 54.0 %all-to-all-start.1 = ((bf16[128,128,128]{2,0,1:T(8,128)(2,1)}), bf16[128,128,128]{2,0,1:T(8,128)(2,1)}, u32[]{:S(2)}, u32[]{:S(2)}) async-start(bf16[128,128,128]{2,0,1:T(8,128)(2,1)} %copy.48), calls=%async_computation.1 | async-start | bytes 8388608 | tf_op jit(solution)/shard_map/all_to_all | solution.py:72
  35.8 47.0 %copy-start.6 = (s32[128]{0:T(128)S(1)}, s32[128]{0:T(128)}, u32[]{:S(2)}) copy-start(s32[128]{0:T(128)} %param.5) | copy-start | bytes 1540
  77.9 52.4 %all-to-all-start.3 = ((bf16[128,128,128]{2,0,1:T(8,128)(2,1)}), bf16[128,128,128]{2,0,1:T(8,128)(2,1)}, u32[]{:S(2)}, u32[]{:S(2)}) async-start(bf16[128,128,128]{2,0,1:T(8,128)(2,1)} %copy.55), calls=%async_computation.3 | async-start | bytes 8388608 | tf_op jit(solution)/shard_map/all_to_all | solution.py:73
  130.3 60.3 %all-to-all-start.2 = ((bf16[128,32,512]{2,1,0:T(8,128)(2,1)}), bf16[128,32,512]{2,1,0:T(8,128)(2,1)}, u32[]{:S(2)}, u32[]{:S(2)}) async-start(bf16[128,32,512]{2,1,0:T(8,128)(2,1)} %broadcast_select_fusion.1), calls=%async_computation.2 | async-start | bytes 8388608 | tf_op jit(solution)/shard_map/all_to_all | solution.py:84
  139.9 205.2 %all-reduce.4.cloned.1.call-start = ((), (), s32[]{:S(2)}) async-start(), calls=%async_computation.4 | async-start | bytes 4194304 | tf_op jit(solution)/shard_map/psum | solution.py:90
  193.5 2.7 copy-start.3
  345.1 1.8 copy-start
  347.1 1.0 copy-start.2
  369.7 121.1 %copy-start.1 = (f32[512,512]{1,0:T(8,128)S(1)}, f32[512,512]{1,0:T(8,128)}, u32[]{:S(2)}) copy-start(f32[512,512]{1,0:T(8,128)} %fusion.18) | copy-start | bytes 3145732
  490.5 5.9 %copy-start.4 = (bf16[64,32,512]{2,1,0:T(8,128)(2,1)S(1)}, bf16[64,32,512]{2,1,0:T(8,128)(2,1)}, u32[]{:S(2)}) copy-start(bf16[64,32,512]{2,1,0:T(8,128)(2,1)} %copy-done.3) | copy-start | bytes 6291460
  496.0 5.5 %copy-start.5 = (f32[512,512]{1,0:T(8,128)S(1)}, f32[512,512]{1,0:T(8,128)}, u32[]{:S(2)}) copy-start(f32[512,512]{1,0:T(8,128)} %get-tuple-element.40) | copy-start | bytes 3145732
Sparse Core Ops, SparseCore 0:
  196.3 148.7 all-reduce.3
where the time goes:
time: 522 us; the launch traced here: 513 us
  waiting for transfers between devices  241 us (46%)
  other arithmetic  131 us (25%)
  local copies, waits for them, and re-layouts  70.2 us (13%)
  starting transfers between devices  28.1 us (5%)
  matrix products  25.6 us (5%)
  between operations  17.2 us (3%)
    psum x1, waiting for transfers between devices, body(): lax.psum((local_gram, local_cross), ('space', 'snap'))  148 us
    another operation x14, other arithmetic, body(): lower = jnp.linalg.cholesky(gram_total / rows_total)  78.9 us
    all_to_all x1, waiting for transfers between devices, body(): lax.all_to_all(owned_x, 'snap', split_axis=1, concat_axis=2, tiled=True)  42.1 us
    another operation x2, other arithmetic, body(): lax.linalg.triangular_solve(lower, identity, left_side=True, lower=True)  40.1 us
    all_to_all x1, waiting for transfers between devices, body(): lax.all_to_all(pick_rows(block_x, outgoing_table), 'space', split_axis=0,...  28.7 us
    all_to_all x1, waiting for transfers between devices, body(): lax.all_to_all(owned_y, 'snap', split_axis=1, concat_axis=2, tiled=True)  22.3 us
    all_to_all x3, local copies, waits for them, and re-layouts, body(): lax.all_to_all(owned_x, 'snap', split_axis=1, concat_axis=2, tiled=True)  19.3 us
    unnamed x17, local copies, waits for them, and re-layouts  16.1 us
  transfers between devices with their start and end apart: 5, of which 4 were waited for; matrix products, arithmetic and copies ran while one was open for 12% of the time, Pallas kernels for 0%

commit v1 on v0

--- a/solution.py
+++ b/solution.py
@@ -87,7 +87,7 @@
     slab_x = jnp.take(moved_x, received_at, axis=0)
     cell_rows = slab_x.reshape(-1, width)
     local_gram = lax.dot_general(cell_rows, cell_rows, contract, preferred_element_type=jnp.float32)
-    gram_total, cross_total = lax.psum((local_gram, local_cross), ("space", "snap"))
+    gram_total, cross_total = lax.psum(lax.psum((local_gram, local_cross), "space"), "snap")
     identity = jnp.eye(width, dtype=jnp.float32)
     lower = jnp.linalg.cholesky(gram_total / rows_total)
     inverse = lax.linalg.triangular_solve(lower, identity, left_side=True, lower=True)

time: 522 us -> 539 us (1.033)
  matrix products: 25.6 us -> 35.8 us
  waiting for transfers between devices: 241 us -> 248 us
    psum x1 -> x2, waiting for transfers between devices: 148 us -> 165 us  [the longest x1 105 us: body(): lax.psum((local_gram, local_cross), 'space')]
    all_to_all x1, waiting for transfers between devices: 28.7 us -> 18.4 us  [body(): lax.all_to_all(pick_rows(block_x, outgoing_table), 'space', split_axis=0,...]
    dot_general x1, matrix products: 3.57 us -> 13.8 us  [body(): lax.dot_general(kept_x.reshape(-1, width), block_y.reshape(-1, width), co...]
  transfers between devices with their start and end apart: 5 -> 6, of which waited for: 4 -> 5; matrix products, arithmetic and copies ran while one was open for 12% -> 14% of each run, Pallas kernels for 0% -> 0%
where the time goes in v1:
time: 539 us; the launch traced here: 530 us
  waiting for transfers between devices  248 us (46%)
  other arithmetic  131 us (24%)
  local copies, waits for them, and re-layouts  70.5 us (13%)
  matrix products  35.8 us (7%)
  starting transfers between devices  28.1 us (5%)
  between operations  17.5 us (3%)
    psum x1, waiting for transfers between devices, body(): lax.psum((local_gram, local_cross), 'space')  105 us
    another operation x14, other arithmetic, body(): lower = jnp.linalg.cholesky(gram_total / rows_total)  78.8 us
    psum x1, waiting for transfers between devices, body(): lax.psum(lax.psum((local_gram, local_cross), 'space'), 'snap')  59.9 us
    all_to_all x1, waiting for transfers between devices, body(): lax.all_to_all(owned_x, 'snap', split_axis=1, concat_axis=2, tiled=True)  42.1 us
    another operation x2, other arithmetic, body(): lax.linalg.triangular_solve(lower, identity, left_side=True, lower=True)  40.1 us
    all_to_all x1, waiting for transfers between devices, body(): lax.all_to_all(owned_y, 'snap', split_axis=1, concat_axis=2, tiled=True)  22.3 us
    all_to_all x3, local copies, waits for them, and re-layouts, body(): lax.all_to_all(owned_x, 'snap', split_axis=1, concat_axis=2, tiled=True)  19.3 us
    all_to_all x1, waiting for transfers between devices, body(): lax.all_to_all(pick_rows(block_x, outgoing_table), 'space', split_axis=0,...  18.4 us
  transfers between devices with their start and end apart: 6, of which 5 were waited for; matrix products, arithmetic and copies ran while one was open for 14% of the time, Pallas kernels for 0%

profile of v1, /device:TPU:1, one launch (start us, length us, event | category | flops | bytes accessed | tf_op | source)
XLA Modules:
  0.0 530.3 jit_solution(18080569921410941893)
XLA Ops:
  8.4 8.6 %all-to-all-start = ((s32[32,1,128]{2,1,0:T(1,128)}), s32[32,1,128]{2,1,0:T(1,128)S(1)}, u32[]{:S(2)}, u32[]{:S(2)}) async-start(s32[32,1,128]{2,1,0:T(1,128)} %broadcast_in_dim.58), calls=%async_computation | async-start | bytes 32768 | tf_op jit(solution)/shard_map/all_to_all | solution.py:19
  17.0 6.9 %copy.48 = bf16[128,128,128]{2,0,1:T(8,128)(2,1)} copy(bf16[128,128,128]{2,1,0:T(8,128)(2,1)} %param.3) | data formatting | bytes 8388608 | tf_op args[0]
  23.9 5.0 all-to-all-start.1
  29.0 6.9 %copy.55 = bf16[128,128,128]{2,0,1:T(8,128)(2,1)} copy(bf16[128,128,128]{2,1,0:T(8,128)(2,1)} %param.4) | data formatting | bytes 8388608 | tf_op args[1]
  35.8 42.1 %all-to-all-done.1 = bf16[128,128,128]{2,0,1:T(8,128)(2,1)} async-done(((bf16[128,128,128]{2,0,1:T(8,128)(2,1)}), bf16[128,128,128]{2,0,1:T(8,128)(2,1)}, u32[]{:S(2)}, u32[]{:S(2)}) %all-to-all-start.1) | async-done | bytes 4194336 | tf_op jit(solution)/shard_map/all_to_all | solution.py:72
  84.0 6.4 %copy.50 = bf16[128,32,4,128]{0,3,2,1:T(8,128)(2,1)} copy(bf16[128,32,4,128]{3,0,1,2:T(8,128)(2,1)} %bitcast.6) | data formatting | bytes 8388608 | tf_op jit(solution)/shard_map/all_to_all | solution.py:72
  90.5 7.9 %copy.51 = bf16[128,32,512]{2,1,0:T(8,128)(2,1)} copy(bf16[128,32,512]{0,2,1:T(8,128)(2,1)} %bitcast.79) | data formatting | bytes 8388608 | tf_op jit(solution)/shard_map/all_to_all | solution.py:72
  108.0 22.3 %all-to-all-done.3 = bf16[128,128,128]{2,0,1:T(8,128)(2,1)} async-done(((bf16[128,128,128]{2,0,1:T(8,128)(2,1)}), bf16[128,128,128]{2,0,1:T(8,128)(2,1)}, u32[]{:S(2)}, u32[]{:S(2)}) %all-to-all-start.3) | async-done | bytes 4194336 | tf_op jit(solution)/shard_map/all_to_all | solution.py:73
  130.3 9.6 %all-to-all-start.2 = ((bf16[128,32,512]{2,1,0:T(8,128)(2,1)}), bf16[128,32,512]{2,1,0:T(8,128)(2,1)}, u32[]{:S(2)}, u32[]{:S(2)}) async-start(bf16[128,32,512]{2,1,0:T(8,128)(2,1)} %broadcast_select_fusion.1), calls=%async_computation.2 | async-start | bytes 8388608 | tf_op jit(solution)/shard_map/all_to_all | solution.py:84
  153.0 5.4 %copy.56 = bf16[128,4,32,128]{3,1,2,0:T(4,128)(2,1)S(1)} copy(bf16[128,4,32,128]{3,0,2,1:T(8,128)(2,1)} %bitcast.23) | data formatting | bytes 8388608 | tf_op jit(solution)/shard_map/all_to_all | solution.py:73
  158.4 13.8 %fusion = f32[512,512]{1,0:T(8,128)} fusion(bf16[512,8,4,128]{3,2,1,0:T(4,128)(2,1)S(1)} %bitcast.81, bf16[512,8,4,128]{3,2,1,0:T(4,128)(2,1)S(1)} %bitcast.80), kind=kOutput, calls=%fused_computation.6 | convolution fusion | flops 2147483648 | bytes 9437184 | tf_op jit(solution)/shard_map/dot_general | solution.py:78
  172.2 18.4 %all-to-all-done.2 = bf16[128,32,512]{2,1,0:T(8,128)(2,1)} async-done(((bf16[128,32,512]{2,1,0:T(8,128)(2,1)}), bf16[128,32,512]{2,1,0:T(8,128)(2,1)}, u32[]{:S(2)}, u32[]{:S(2)}) %all-to-all-start.2) | async-done | bytes 4194336 | tf_op jit(solution)/shard_map/all_to_all | solution.py:84
  196.2 104.9 %all-reduce.6.cloned.1.call-done = (f32[512,512]{0,1:T(8,128)}, f32[512,512]{1,0:T(8,128)}) async-done(((f32[512,512]{0,1:T(8,128)}, f32[512,512]{1,0:T(8,128)}), (f32[512,512]{0,1:T(8,128)}, f32[512,512]{1,0:T(8,128)})) %all-reduce.6.cloned.1.call-update) | async-done | bytes 2097168 | tf_op jit(solution)/shard_map/psum | solution.py:90
  302.4 59.9 %all-reduce.8.cloned.1.call-done = (f32[512,512]{0,1:T(8,128)}, f32[512,512]{1,0:T(8,128)}) async-done(((f32[512,512]{0,1:T(8,128)}, f32[512,512]{1,0:T(8,128)}), (f32[512,512]{0,1:T(8,128)}, f32[512,512]{1,0:T(8,128)})) %all-reduce.8.cloned.1.call-update) | async-done | bytes 2097168 | tf_op jit(solution)/shard_map/psum | solution.py:90
  365.2 11.7 %cholesky.96 = f32[128,128]{1,0:T(8,128)S(1)} custom-call(f32[128,128]{1,0:T(8,128)S(1)} %cholesky.250), custom_call_target="Cholesky" | custom-call | tf_op jit(solution)/shard_map/jit(cholesky)/cholesky | solution.py:92
  377.0 9.8 %custom-call.30 = f32[1,128,128]{1,2,0:T(8,128)S(1)} custom-call(f32[1,128,128]{2,1,0:T(8,128)S(1)} %get-tuple-element.58), custom_call_target="InvertDiagBlocksLowerTriangular" | custom-call | tf_op jit(solution)/shard_map/jit(cholesky)/cholesky | solution.py:92
  389.6 11.7 %cholesky.201 = f32[128,128]{1,0:T(8,128)S(1)} custom-call(f32[128,128]{1,0:T(8,128)S(1)} %cholesky.254), custom_call_target="Cholesky" | custom-call | tf_op jit(solution)/shard_map/jit(cholesky)/cholesky | solution.py:92
  401.3 10.0 %custom-call.31 = f32[1,128,128]{1,2,0:T(8,128)S(1)} custom-call(f32[1,128,128]{2,1,0:T(8,128)S(1)} %get-tuple-element.55), custom_call_target="InvertDiagBlocksLowerTriangular" | custom-call | tf_op jit(solution)/shard_map/jit(cholesky)/cholesky | solution.py:92
  412.9 11.7 %cholesky.222 = f32[128,128]{1,0:T(8,128)S(1)} custom-call(f32[128,128]{1,0:T(8,128)S(1)} %cholesky.259), custom_call_target="Cholesky" | custom-call | tf_op jit(solution)/shard_map/jit(cholesky)/cholesky | solution.py:92
  425.3 9.8 %custom-call.32 = f32[1,128,128]{1,2,0:T(8,128)S(1)} custom-call(f32[1,128,128]{2,1,0:T(8,128)S(1)} %get-tuple-element.52), custom_call_target="InvertDiagBlocksLowerTriangular" | custom-call | tf_op jit(solution)/shard_map/jit(cholesky)/cholesky | solution.py:92
  436.6 11.9 %cholesky.239 = f32[128,128]{1,0:T(8,128)S(1)} custom-call(f32[128,128]{1,0:T(8,128)S(1)} %convolution_subtract_fusion.5), custom_call_target="Cholesky" | custom-call | tf_op jit(solution)/shard_map/jit(cholesky)/cholesky | solution.py:92
  453.6 14.1 %while.1 = (s32[]{:T(128)}, f32[512,512]{1,0:T(8,128)}, s32[4,2]{0,1:T(2,128)S(1)}, f32[4,128,128]{2,1,0:T(8,128)}, s32[]{:T(128)}) while((s32[]{:T(128)}, f32[512,512]{1,0:T(8,128)}, s32[4,2]{0,1:T(2,128)S(1)}, f32[4,128,128]{2,1,0:T(8,128)}, s32[]{:T(128)}) %tuple.41), condition=%wide.while_cond, body=%wide.while_body.sunk | while | flops 2 | bytes 132705 | solution.py:93
  467.8 40.1 %custom-call.33 = f32[4,128,128]{1,2,0:T(8,128)S(1)} custom-call(f32[4,128,128]{2,1,0:T(8,128)} %get-tuple-element.12), custom_call_target="InvertDiagBlocksLowerTriangular" | custom-call | tf_op jit(solution)/shard_map/triangular_solve | solution.py:93
  513.8 5.1 fusion.5
  (95 shorter events, 72.8 us)
Async XLA Ops:
  8.4 15.5 %all-to-all-start = ((s32[32,1,128]{2,1,0:T(1,128)}), s32[32,1,128]{2,1,0:T(1,128)S(1)}, u32[]{:S(2)}, u32[]{:S(2)}) async-start(s32[32,1,128]{2,1,0:T(1,128)} %broadcast_in_dim.58), calls=%async_computation | async-start | bytes 32768 | tf_op jit(solution)/shard_map/all_to_all | solution.py:19
  23.9 54.0 %all-to-all-start.1 = ((bf16[128,128,128]{2,0,1:T(8,128)(2,1)}), bf16[128,128,128]{2,0,1:T(8,128)(2,1)}, u32[]{:S(2)}, u32[]{:S(2)}) async-start(bf16[128,128,128]{2,0,1:T(8,128)(2,1)} %copy.48), calls=%async_computation.1 | async-start | bytes 8388608 | tf_op jit(solution)/shard_map/all_to_all | solution.py:72
  35.8 47.0 %copy-start.6 = (s32[128]{0:T(128)S(1)}, s32[128]{0:T(128)}, u32[]{:S(2)}) copy-start(s32[128]{0:T(128)} %param.5) | copy-start | bytes 1540
  77.9 52.4 %all-to-all-start.3 = ((bf16[128,128,128]{2,0,1:T(8,128)(2,1)}), bf16[128,128,128]{2,0,1:T(8,128)(2,1)}, u32[]{:S(2)}, u32[]{:S(2)}) async-start(bf16[128,128,128]{2,0,1:T(8,128)(2,1)} %copy.55), calls=%async_computation.3 | async-start | bytes 8388608 | tf_op jit(solution)/shard_map/all_to_all | solution.py:73
  130.3 60.3 %all-to-all-start.2 = ((bf16[128,32,512]{2,1,0:T(8,128)(2,1)}), bf16[128,32,512]{2,1,0:T(8,128)(2,1)}, u32[]{:S(2)}, u32[]{:S(2)}) async-start(bf16[128,32,512]{2,1,0:T(8,128)(2,1)} %broadcast_select_fusion.1), calls=%async_computation.2 | async-start | bytes 8388608 | tf_op jit(solution)/shard_map/all_to_all | solution.py:84
  139.9 161.2 %all-reduce.6.cloned.1.call-start = ((), (), s32[]{:S(2)}) async-start(), calls=%async_computation.4 | async-start | bytes 4194304 | tf_op jit(solution)/shard_map/psum | solution.py:90
  193.5 2.7 copy-start.3
  196.2 166.1 %all-reduce.8.cloned.1.call-start = ((), (), s32[]{:S(2)}) async-start(), calls=%async_computation.5 | async-start | bytes 4194304 | tf_op jit(solution)/shard_map/psum | solution.py:90
  362.3 1.8 copy-start
  364.3 1.0 copy-start.2
  386.9 121.3 %copy-start.1 = (f32[512,512]{1,0:T(8,128)S(1)}, f32[512,512]{1,0:T(8,128)}, u32[]{:S(2)}) copy-start(f32[512,512]{1,0:T(8,128)} %fusion.18) | copy-start | bytes 3145732
  507.9 5.9 %copy-start.4 = (bf16[64,32,512]{2,1,0:T(8,128)(2,1)S(1)}, bf16[64,32,512]{2,1,0:T(8,128)(2,1)}, u32[]{:S(2)}) copy-start(bf16[64,32,512]{2,1,0:T(8,128)(2,1)} %copy-done.3) | copy-start | bytes 6291460
  513.4 5.5 %copy-start.5 = (f32[512,512]{1,0:T(8,128)S(1)}, f32[512,512]{1,0:T(8,128)}, u32[]{:S(2)}) copy-start(f32[512,512]{1,0:T(8,128)} %get-tuple-element.42) | copy-start | bytes 3145732
Sparse Core Ops, SparseCore 0:
  196.3 104.8 all-reduce.5
  303.6 58.6 all-reduce.7
